TPU v7x, 32 devices: a whole 2x2x4 slice. The times are simulated.
32 devices in a mesh: rep: 2 (over y), span: 2 (over x), seq: 4 (over z), head: 2 (over core).
Axes of the slice: x: 2, y: 2, z: 4, core: 2. Of those that a mesh axis runs over, the one named last changes fastest.
Arguments:
- queries: bfloat16 [4, 2, 1024, 4096], P(('rep', 'span'), 'head', None, 'seq'), parts along dimension 0, may hold values from -12 to 12
- keys: bfloat16 [4, 2, 1024, 4096], P(('rep', 'span'), 'head', None, 'seq'), parts along dimension 0, may hold values from -12 to 12
- values: bfloat16 [4, 2, 1024, 4096], P(('rep', 'span'), 'head', None, 'seq'), parts along dimension 0, may hold values from -6 to 6
- span_order: int32 [4], P('rep'), parts along dimension 0, may hold values from 0 to 15, as said below
Outputs:
- attention: bfloat16 [4, 2, 1024, 4096], P(('rep', 'span'), 'head', 'seq'), parts along dimension 0
There are 2 independent parts, one for each index of `rep`. A program takes and returns all parts, laid end to end along the dimension named above; each array names one. Nothing has to cross between parts.
Inputs may be any that keep to these rules, and one draw needn't show every extreme that they name: `span_order`: each group has a different span index.
All inputs are finite; a program needn't handle non-finite values.
Results may differ from a plain program's by a relative error of at most 0.0055.
Values may be sent and summed in bfloat16 or wider, within the bound.
A program may use at most 128 MiB of HBM per device.

v0:
```python
import math

import jax
import jax.numpy as jnp
from jax import lax
from jax.sharding import PartitionSpec as P

HD = 128


def lookup(span_order, block_index):
    table = jnp.arange(span_order.shape[0], dtype=jnp.int32)
    return jnp.sum(
        jnp.where(block_index[:, None] == table[None, :], span_order[None, :], 0), axis=1
    )


def initial(query_heads):
    query_count = query_heads.shape[0]
    local_heads = query_heads.shape[1]
    return (
        jnp.full((local_heads, query_count), -1e30, jnp.float32),
        jnp.zeros((local_heads, query_count), jnp.float32),
        jnp.zeros((local_heads, query_count, HD), jnp.float32),
    )


def attend(running, query_heads, key_piece, value_piece, block_span, own_span, bias_rate):
    block_count = key_piece.shape[0]
    piece_rows = key_piece.shape[1]
    local_heads = key_piece.shape[2] // HD
    key_count = block_count * piece_rows
    score_scale = 1.0 / math.sqrt(HD)
    key_spans = jnp.repeat(block_span, piece_rows)
    allowed = key_spans <= own_span
    distance_bias = (own_span - key_spans).astype(jnp.float32) * jnp.float32(bias_rate)
    block_size = 1024
    block_total = key_count // block_size
    key_blocks = key_piece.reshape(block_total, block_size, local_heads, HD)
    value_blocks = value_piece.reshape(block_total, block_size, local_heads, HD)
    allow_blocks = allowed.reshape(block_total, block_size)
    bias_blocks = distance_bias.reshape(block_total, block_size)

    def advance(status, block_item):
        key_block, value_block, allow_block, bias_block = block_item
        maxima, totals, weighted = status
        scores = (
            jnp.einsum("qhd,khd->hqk", query_heads, key_block, preferred_element_type=jnp.float32)
            * score_scale
        )
        scores = scores - bias_block[None, None, :]
        scores = jnp.where(allow_block[None, None, :], scores, jnp.float32(-1e30))
        new_max = jnp.maximum(maxima, jnp.max(scores, axis=2))
        weights = jnp.where(
            allow_block[None, None, :], jnp.exp(scores - new_max[:, :, None]), 0.0
        ).astype(jnp.bfloat16)
        shrink = jnp.exp(maxima - new_max)
        totals = totals * shrink + jnp.sum(weights.astype(jnp.float32), axis=2)
        weighted = weighted * shrink[:, :, None] + jnp.einsum(
            "hqk,khd->hqd", weights, value_block, preferred_element_type=jnp.float32
        )
        return ((new_max, totals, weighted), None)

    running, unused = lax.scan(
        advance, running, (key_blocks, value_blocks, allow_blocks, bias_blocks)
    )
    return running


def finish(running):
    maxima, totals, weighted = running
    local_heads = weighted.shape[0]
    query_count = weighted.shape[1]
    output = (weighted / totals[:, :, None]).transpose(1, 0, 2)
    return output.reshape(1, 1, query_count, local_heads * HD).astype(jnp.bfloat16)


def per_device(queries, keys, values, span_order):
    half_rows = queries.shape[2]
    local_width = queries.shape[3]
    local_heads = local_width // HD
    halves = lax.axis_size("head")
    bias_rate = 1.0 / (2.0 * span_order.shape[0])
    own_span = lookup(span_order, jnp.reshape(lax.axis_index("span"), (1,)))[0]
    query_heads = queries.reshape(half_rows, local_heads, HD)
    pieces = (
        lax.all_gather(keys, ("span", "head"), axis=0, tiled=True),
        lax.all_gather(values, ("span", "head"), axis=0, tiled=True),
    )
    count = pieces[0].shape[0]
    block_index = jnp.arange(count, dtype=jnp.int32) // halves
    key_piece = pieces[0].reshape(count, half_rows, local_width)
    value_piece = pieces[1].reshape(count, half_rows, local_width)
    running = attend(
        initial(query_heads),
        query_heads,
        key_piece,
        value_piece,
        lookup(span_order, block_index),
        own_span,
        bias_rate,
    )
    result = finish(running)
    return lax.all_to_all(result, "seq", split_axis=2, concat_axis=3, tiled=True)


def solution(mesh):
    return jax.shard_map(
        per_device,
        mesh=mesh,
        in_specs=(
            P(("rep", "span"), "head", None, "seq"),
            P(("rep", "span"), "head", None, "seq"),
            P(("rep", "span"), "head", None, "seq"),
            P("rep"),
        ),
        out_specs=P(("rep", "span"), "head", "seq", None),
        check_vma=False,
    )
```

profile of v0, /device:TPU:0, one launch (start us, length us, event | category | flops | bytes accessed | tf_op | source)
XLA Modules:
  0.0 445.6 jit_solution(3276279276303057130)
XLA Ops:
  15.2 54.7 %all-gather.3.cloned.1.call-done = bf16[4,1,1024,1024]{3,2,1,0:T(8,128)(2,1)} async-done(((bf16[1,1,1024,1024]{3,2,1,0:T(8,128)(2,1)}), bf16[4,1,1024,1024]{3,2,1,0:T(8,128)(2,1)}) %all-gather.3.cloned.1.call-update) | async-done | bytes 8388624 | tf_op jit(solution)/shard_map/all_gather | solution.py:87
  69.9 11.6 %copy.38 = bf16[4,1,1024,1024]{2,3,0,1:T(8,128)(2,1)} copy(bf16[4,1,1024,1024]{3,2,1,0:T(8,128)(2,1)} %all-gather.3.cloned.1.call-done) | data formatting | bytes 16777216 | tf_op jit(solution)/shard_map/all_gather | solution.py:87
  81.5 48.2 %all-gather.5.cloned.1.call-done = bf16[4,1,1024,1024]{3,2,1,0:T(8,128)(2,1)} async-done(((bf16[1,1,1024,1024]{3,2,1,0:T(8,128)(2,1)}), bf16[4,1,1024,1024]{3,2,1,0:T(8,128)(2,1)}) %all-gather.5.cloned.1.call-update) | async-done | bytes 8388624 | tf_op jit(solution)/shard_map/all_gather | solution.py:88
  129.8 11.4 %copy.40 = bf16[4,1,1024,1024]{2,3,0,1:T(8,128)(2,1)} copy(bf16[4,1,1024,1024]{3,2,1,0:T(8,128)(2,1)} %all-gather.5.cloned.1.call-done) | data formatting | bytes 16777216 | tf_op jit(solution)/shard_map/all_gather | solution.py:88
  141.3 199.1 %while.15 = (s32[]{:T(128)}, f32[8,1024]{1,0:T(8,128)S(1)}, f32[8,1024]{1,0:T(8,128)S(1)}, f32[8,1024,128]{2,1,0:T(8,128)}, pred[4,1024]{1,0:T(4,128)(4,1)S(1)},...) while((s32[]{:T(128)}, f32[8,1024]{1,0:T(8,128)S(1)}, ...), condition=%wide.region_5.6_spmd.clone, body=%wide.region_2.5_spmd.clone.sunk | while | flops 4398817280 | bytes 115856512 | solution.py:64
  141.3 16.6 %bitcast_reduce_fusion.2 = (f32[8,1024]{1,0:T(8,128)S(1)}, f32[8,1024,1024]{2,1,0:T(8,128)}) fusion(f32[1024]{0:T(1024)S(1)} %bitcast.57, pred[1024]{0:T(1024)(128)(4,1)S(1)} %dynamic-slice_reduce_fusion.2, bf16[1024,8,128]{2,0,1:T(8,128)(2,1)S(1)} %get-tuple-element.240, bf16[4,1024,8,128]{1,3,2,0:T(8,128)(2,1)} %get-tuple-element.239, ...), kind=kOutput, calls=%fused_computation.1.clone.1 | convolution fusion | flops 2181029888 | bytes 37787136 | tf_op jit(solution)/shard_map/while/body/eval_jaxpr/qhd,khd->hqk/dot_general | solution.py:48
  157.9 21.6 %convert_reduce_fusion.2 = (f32[8,1024]{1,0:T(8,128)S(1)}, bf16[8,1024,1024]{1,2,0:T(8,128)(2,1)}) fusion(f32[8,1024]{1,0:T(8,128)S(1)} %select_maximum_fusion.2, f32[1024]{0:T(1024)S(1)} %bitcast.58, f32[8,1024,1024]{2,1,0:T(8,128)} %get-tuple-element.207, pred[1024]{0:T(1024)(128)(4,1)S(1)} %dynamic-slice_reduce_fusion.2), kind=kLoop, calls=%fused_computation.5.clone.1 | loop fusion | flops 67100672 | bytes 50402304 | tf_op jit(solution)/shard_map/while/body/eval_jaxpr/reduce_sum | solution.py:58
  179.5 11.0 %fusion.29 = f32[8,1024,128]{2,1,0:T(8,128)} fusion(f32[8,1024,128]{2,1,0:T(8,128)} %get-tuple-element.226, f32[8,1024]{1,0:T(8,128)S(1)} %get-tuple-element.210, pred[]{:T(512)S(6)} %compare.7, bf16[8,1024,1024]{1,2,0:T(8,128)(2,1)} %get-tuple-element.211, bf16[4,1024,8,128]{1,3,2,0:T(8,128)(2,1)} %get-tuple-element.242, s32[]{:T(128)} %get-tuple-element.223), kind=kOutput, calls=%fused_computation.8.clone.1 | convolution fusion | flops 2150629376 | bytes 27296256 | tf_op jit(solution)/shard_map/while/body/eval_jaxpr/hqk,khd->hqd/dot_general | solution.py:59
  190.5 16.6 %bitcast_reduce_fusion.2 = (f32[8,1024]{1,0:T(8,128)S(1)}, f32[8,1024,1024]{2,1,0:T(8,128)}) fusion(f32[1024]{0:T(1024)S(1)} %bitcast.57, pred[1024]{0:T(1024)(128)(4,1)S(1)} %dynamic-slice_reduce_fusion.2, bf16[1024,8,128]{2,0,1:T(8,128)(2,1)S(1)} %get-tuple-element.240, bf16[4,1024,8,128]{1,3,2,0:T(8,128)(2,1)} %get-tuple-element.239, ...), kind=kOutput, calls=%fused_computation.1.clone.1 | convolution fusion | flops 2181029888 | bytes 37787136 | tf_op jit(solution)/shard_map/while/body/eval_jaxpr/qhd,khd->hqk/dot_general | solution.py:48
  207.1 21.6 %convert_reduce_fusion.2 = (f32[8,1024]{1,0:T(8,128)S(1)}, bf16[8,1024,1024]{1,2,0:T(8,128)(2,1)}) fusion(f32[8,1024]{1,0:T(8,128)S(1)} %select_maximum_fusion.2, f32[1024]{0:T(1024)S(1)} %bitcast.58, f32[8,1024,1024]{2,1,0:T(8,128)} %get-tuple-element.207, pred[1024]{0:T(1024)(128)(4,1)S(1)} %dynamic-slice_reduce_fusion.2), kind=kLoop, calls=%fused_computation.5.clone.1 | loop fusion | flops 67100672 | bytes 50402304 | tf_op jit(solution)/shard_map/while/body/eval_jaxpr/reduce_sum | solution.py:58
  228.7 11.7 %fusion.29 = f32[8,1024,128]{2,1,0:T(8,128)} fusion(f32[8,1024,128]{2,1,0:T(8,128)} %get-tuple-element.226, f32[8,1024]{1,0:T(8,128)S(1)} %get-tuple-element.210, pred[]{:T(512)S(6)} %compare.7, bf16[8,1024,1024]{1,2,0:T(8,128)(2,1)} %get-tuple-element.211, bf16[4,1024,8,128]{1,3,2,0:T(8,128)(2,1)} %get-tuple-element.242, s32[]{:T(128)} %get-tuple-element.223), kind=kOutput, calls=%fused_computation.8.clone.1 | convolution fusion | flops 2150629376 | bytes 27296256 | tf_op jit(solution)/shard_map/while/body/eval_jaxpr/hqk,khd->hqd/dot_general | solution.py:59
  240.5 16.6 %bitcast_reduce_fusion.2 = (f32[8,1024]{1,0:T(8,128)S(1)}, f32[8,1024,1024]{2,1,0:T(8,128)}) fusion(f32[1024]{0:T(1024)S(1)} %bitcast.57, pred[1024]{0:T(1024)(128)(4,1)S(1)} %dynamic-slice_reduce_fusion.2, bf16[1024,8,128]{2,0,1:T(8,128)(2,1)S(1)} %get-tuple-element.240, bf16[4,1024,8,128]{1,3,2,0:T(8,128)(2,1)} %get-tuple-element.239, ...), kind=kOutput, calls=%fused_computation.1.clone.1 | convolution fusion | flops 2181029888 | bytes 37787136 | tf_op jit(solution)/shard_map/while/body/eval_jaxpr/qhd,khd->hqk/dot_general | solution.py:48
  257.1 21.6 %convert_reduce_fusion.2 = (f32[8,1024]{1,0:T(8,128)S(1)}, bf16[8,1024,1024]{1,2,0:T(8,128)(2,1)}) fusion(f32[8,1024]{1,0:T(8,128)S(1)} %select_maximum_fusion.2, f32[1024]{0:T(1024)S(1)} %bitcast.58, f32[8,1024,1024]{2,1,0:T(8,128)} %get-tuple-element.207, pred[1024]{0:T(1024)(128)(4,1)S(1)} %dynamic-slice_reduce_fusion.2), kind=kLoop, calls=%fused_computation.5.clone.1 | loop fusion | flops 67100672 | bytes 50402304 | tf_op jit(solution)/shard_map/while/body/eval_jaxpr/reduce_sum | solution.py:58
  278.7 11.7 %fusion.29 = f32[8,1024,128]{2,1,0:T(8,128)} fusion(f32[8,1024,128]{2,1,0:T(8,128)} %get-tuple-element.226, f32[8,1024]{1,0:T(8,128)S(1)} %get-tuple-element.210, pred[]{:T(512)S(6)} %compare.7, bf16[8,1024,1024]{1,2,0:T(8,128)(2,1)} %get-tuple-element.211, bf16[4,1024,8,128]{1,3,2,0:T(8,128)(2,1)} %get-tuple-element.242, s32[]{:T(128)} %get-tuple-element.223), kind=kOutput, calls=%fused_computation.8.clone.1 | convolution fusion | flops 2150629376 | bytes 27296256 | tf_op jit(solution)/shard_map/while/body/eval_jaxpr/hqk,khd->hqd/dot_general | solution.py:59
  290.5 16.6 %bitcast_reduce_fusion.2 = (f32[8,1024]{1,0:T(8,128)S(1)}, f32[8,1024,1024]{2,1,0:T(8,128)}) fusion(f32[1024]{0:T(1024)S(1)} %bitcast.57, pred[1024]{0:T(1024)(128)(4,1)S(1)} %dynamic-slice_reduce_fusion.2, bf16[1024,8,128]{2,0,1:T(8,128)(2,1)S(1)} %get-tuple-element.240, bf16[4,1024,8,128]{1,3,2,0:T(8,128)(2,1)} %get-tuple-element.239, ...), kind=kOutput, calls=%fused_computation.1.clone.1 | convolution fusion | flops 2181029888 | bytes 37787136 | tf_op jit(solution)/shard_map/while/body/eval_jaxpr/qhd,khd->hqk/dot_general | solution.py:48
  307.0 21.6 %convert_reduce_fusion.2 = (f32[8,1024]{1,0:T(8,128)S(1)}, bf16[8,1024,1024]{1,2,0:T(8,128)(2,1)}) fusion(f32[8,1024]{1,0:T(8,128)S(1)} %select_maximum_fusion.2, f32[1024]{0:T(1024)S(1)} %bitcast.58, f32[8,1024,1024]{2,1,0:T(8,128)} %get-tuple-element.207, pred[1024]{0:T(1024)(128)(4,1)S(1)} %dynamic-slice_reduce_fusion.2), kind=kLoop, calls=%fused_computation.5.clone.1 | loop fusion | flops 67100672 | bytes 50402304 | tf_op jit(solution)/shard_map/while/body/eval_jaxpr/reduce_sum | solution.py:58
  328.7 11.7 %fusion.29 = f32[8,1024,128]{2,1,0:T(8,128)} fusion(f32[8,1024,128]{2,1,0:T(8,128)} %get-tuple-element.226, f32[8,1024]{1,0:T(8,128)S(1)} %get-tuple-element.210, pred[]{:T(512)S(6)} %compare.7, bf16[8,1024,1024]{1,2,0:T(8,128)(2,1)} %get-tuple-element.211, bf16[4,1024,8,128]{1,3,2,0:T(8,128)(2,1)} %get-tuple-element.242, s32[]{:T(128)} %get-tuple-element.223), kind=kOutput, calls=%fused_computation.8.clone.1 | convolution fusion | flops 2150629376 | bytes 27296256 | tf_op jit(solution)/shard_map/while/body/eval_jaxpr/hqk,khd->hqd/dot_general | solution.py:59
  340.4 5.4 %copy.44 = f32[8,1024,128]{1,2,0:T(8,128)} copy(f32[8,1024,128]{2,1,0:T(8,128)} %get-tuple-element.53) | data formatting | bytes 8388608 | tf_op jit(solution)/shard_map/while | solution.py:64
  348.6 7.7 %copy.45 = bf16[1,1,1024,1024]{3,1,0,2:T(2,128)(2,1)} copy(bf16[1,1,1024,1024]{2,3,1,0:T(8,128)(2,1)S(1)} %bitcast.51) | data formatting | bytes 4194304 | tf_op jit(solution)/shard_map/convert_element_type | solution.py:75
  356.8 13.0 %reduce.4 = bf16[1024,1024]{1,0:T(8,128)(2,1)S(1)} reduce(bf16[1024,1,1,1024]{3,2,1,0:T(2,128)(2,1)} %bitcast.49, bf16[]{:T(256)} %broadcast.88), dimensions={1,2}, to_apply=%bitcast.30.reduce_sub_computation | reduce | bytes 4194306
  372.6 53.2 %all_to_all.18 = bf16[4,2,131072]{2,1,0:T(2,128)(2,1)S(1)} all-to-all(bf16[4,2,131072]{2,1,0:T(2,128)(2,1)} %reshape.51), channel_id=1, replica_groups=mesh['rep'=2,'span'=2,'seq'=4,'head'=2] {'seq'}, dimensions={0} | all-to-all | bytes 4194304 | tf_op jit(solution)/shard_map/all_to_all | solution.py:104
  425.8 3.4 reshape.52
  429.1 3.0 copy.51
  434.7 4.1 copy.47
  (44 shorter events, 17.6 us)
Async XLA Ops:
  6.5 63.4 %all-gather.3.cloned.1.call-start = ((), (), s32[]{:S(2)}) async-start(), calls=%async_computation.1 | async-start | bytes 10485760 | tf_op jit(solution)/shard_map/all_gather | solution.py:87
  7.3 122.5 %all-gather.5.cloned.1.call-start = ((), (), s32[]{:S(2)}) async-start(), calls=%async_computation.2 | async-start | bytes 10485760 | tf_op jit(solution)/shard_map/all_gather | solution.py:88
  8.0 5.3 %copy-start.1 = (s32[2]{0:T(128)S(1)}, s32[2]{0:T(128)}, u32[]{:S(2)}) copy-start(s32[2]{0:T(128)} %param.9) | copy-start | bytes 28
  81.5 59.7 %copy-start = (bf16[1024,8,128]{2,0,1:T(8,128)(2,1)S(1)}, bf16[1024,8,128]{2,0,1:T(8,128)(2,1)}, u32[]{:S(2)}) copy-start(bf16[1024,8,128]{2,0,1:T(8,128)(2,1)} %copy.42) | copy-start | bytes 6291460
Sparse Core Ops, SparseCore 0:
  8.9 60.9 all-gather.2
  71.5 58.2 all-gather.4
where the time goes:
time: 447 us; the launch traced here: 446 us
  matrix products  112 us (25%)
  waiting for transfers between devices  104 us (23%)
  other arithmetic  104 us (23%)
  local copies, waits for them, and re-layouts  57.9 us (13%)
  blocking collectives  53.2 us (12%)
  between operations  13.5 us (3%)
    reduce_sum x4, other arithmetic, advance(): totals = totals * shrink + jnp.sum(weights.astype(jnp.float32), axis=2)  86.4 us
    dot_general x4, matrix products, advance(): jnp.einsum('qhd,khd->hqk', query_heads, key_block, preferred_element_type...  66.3 us
    all_gather x1, waiting for transfers between devices, per_device(): lax.all_gather(keys, ('span', 'head'), axis=0, tiled=True)  54.7 us
    all_to_all x1, blocking collectives, per_device(): lax.all_to_all(result, 'seq', split_axis=2, concat_axis=3, tiled=True)  53.2 us
    all_gather x1, waiting for transfers between devices, per_device(): lax.all_gather(values, ('span', 'head'), axis=0, tiled=True)  48.2 us
    dot_general x4, matrix products, advance(): jnp.einsum('hqk,khd->hqd', weights, value_block, preferred_element_type=j...  46.2 us
    unnamed x10, local copies, waits for them, and re-layouts  14.9 us
    unnamed x4, other arithmetic  13 us
  transfers between devices with their start and end apart: 2, of which 2 were waited for; matrix products, arithmetic and copies ran while one was open for 4% of the time, Pallas kernels for 0%

commit v1 on v0

--- a/solution.py
+++ b/solution.py
@@ -1,8 +1,11 @@
+import functools
 import math
 
 import jax
 import jax.numpy as jnp
 from jax import lax
+from jax.experimental import pallas as pl
+from jax.experimental.pallas import tpu as pltpu
 from jax.sharding import PartitionSpec as P
 
 HD = 128
@@ -75,7 +78,7 @@
     return output.reshape(1, 1, query_count, local_heads * HD).astype(jnp.bfloat16)
 
 
-def per_device(queries, keys, values, span_order):
+def per_device_general(queries, keys, values, span_order):
     half_rows = queries.shape[2]
     local_width = queries.shape[3]
     local_heads = local_width // HD
@@ -104,6 +107,200 @@
     return lax.all_to_all(result, "seq", split_axis=2, concat_axis=3, tiled=True)
 
 
+MESH = pl.DeviceIdType.MESH
+ROWS = 256
+LOG2E = 1.4426950408889634
+
+
+def fused_kernel(
+    heads, seq_count, shift_ref, q_ref, k_ref, v_ref, out_ref,
+    kp, vp, kx, vx, kd, vd, stage,
+    p_send, p_recv, x_send, x_recv, d_send, d_recv, z_send, z_recv, own_sem,
+):
+    rep, span = lax.axis_index("rep"), lax.axis_index("span")
+    seq, core = lax.axis_index("seq"), lax.axis_index("head")
+    partner = (rep, span, seq, 1 - core)
+    across = (rep, 1 - span, seq, core)
+    tokens, width = q_ref.shape
+    part = tokens // seq_count
+
+    def along(step):
+        return lax.rem(seq + step, seq_count)
+
+    barrier = pltpu.get_barrier_semaphore()
+    peers = [partner, across] + [(rep, span, along(i), core) for i in range(1, seq_count)]
+    for peer in peers:
+        pl.semaphore_signal(barrier, inc=1, device_id=peer, device_id_type=MESH)
+    pl.semaphore_wait(barrier, len(peers))
+
+    def cols(h):
+        return pl.ds(pl.multiple_of(h * HD, HD), HD)
+
+    def move(src, dst, send, recv, which, h, device):
+        return pltpu.make_async_remote_copy(
+            src_ref=src.at[:, cols(h)],
+            dst_ref=dst.at[:, cols(h)],
+            send_sem=send.at[which, h],
+            recv_sem=recv.at[which, h],
+            device_id=device,
+            device_id_type=MESH,
+        )
+
+    def to_across(h):
+        return (
+            move(k_ref, kx, x_send, x_recv, 0, h, across),
+            move(v_ref, vx, x_send, x_recv, 1, h, across),
+        )
+
+    def to_partner(h):
+        return (
+            move(k_ref, kp, p_send, p_recv, 0, h, partner),
+            move(v_ref, vp, p_send, p_recv, 1, h, partner),
+        )
+
+    def relay(h):
+        return (
+            move(kx, kd, d_send, d_recv, 0, h, partner),
+            move(vx, vd, d_send, d_recv, 1, h, partner),
+        )
+
+    def out_cols(from_seq, h):
+        return pl.ds(pl.multiple_of(from_seq * width + h * HD, HD), HD)
+
+    def to_seq(h, step):
+        target = along(step)
+        return pltpu.make_async_remote_copy(
+            src_ref=stage.at[pl.ds(pl.multiple_of(target * part, part), part), cols(h)],
+            dst_ref=out_ref.at[:, out_cols(seq, h)],
+            send_sem=z_send.at[step - 1, h],
+            recv_sem=z_recv.at[step - 1, h],
+            device_id=(rep, span, target, core),
+            device_id_type=MESH,
+        )
+
+    def to_self(h):
+        return pltpu.make_async_copy(
+            stage.at[pl.ds(pl.multiple_of(seq * part, part), part), cols(h)],
+            out_ref.at[:, out_cols(seq, h)],
+            own_sem.at[h],
+        )
+
+    def launch(h, carry):
+        for copy in to_across(h) + to_partner(h):
+            copy.start()
+        return carry
+
+    lax.fori_loop(0, heads, launch, 0)
+
+    rate = jnp.float32(LOG2E / math.sqrt(HD))
+    shift = shift_ref[0]
+
+    def one_head(h, carry):
+        for copy in to_across(h):
+            copy.wait_recv()
+        for copy in relay(h):
+            copy.start()
+        for copy in to_partner(h):
+            copy.wait_recv()
+        for copy in relay(h):
+            copy.wait_recv()
+
+        def tile(t, inner):
+            rows = pl.ds(pl.multiple_of(t * ROWS, ROWS), ROWS)
+            query = q_ref[rows, cols(h)]
+
+            def score(ref):
+                return lax.dot_general(
+                    query, ref[:, cols(h)], (((1,), (1,)), ((), ())),
+                    preferred_element_type=jnp.float32,
+                )
+
+            near = [score(k_ref), score(kp)]
+            far = [score(kx), score(kd)]
+            near_max = jnp.max(jnp.maximum(near[0], near[1]), axis=1, keepdims=True) * rate
+            far_max = jnp.max(jnp.maximum(far[0], far[1]), axis=1, keepdims=True) * rate
+            top = jnp.maximum(near_max, far_max - shift)
+            far_top = top + shift
+            total = None
+            ones = jnp.ones((tokens, HD), jnp.bfloat16)
+            for scores, offset, ref in (
+                (near[0], top, v_ref), (near[1], top, vp),
+                (far[0], far_top, vx), (far[1], far_top, vd),
+            ):
+                weights = jnp.exp2(scores * rate - offset).astype(jnp.bfloat16)
+                value = jnp.concatenate([ref[:, cols(h)], ones], axis=1)
+                term = jnp.dot(weights, value, preferred_element_type=jnp.float32)
+                total = term if total is None else total + term
+            stage[rows, cols(h)] = (total[:, :HD] / total[:, HD:]).astype(jnp.bfloat16)
+            return inner
+
+        lax.fori_loop(0, tokens // ROWS, tile, 0)
+        for step in range(1, seq_count):
+            to_seq(h, step).start()
+        to_self(h).start()
+        return carry
+
+    lax.fori_loop(0, heads, one_head, 0)
+
+    def drain(h, carry):
+        for copy in to_across(h) + to_partner(h) + relay(h):
+            copy.wait_send()
+        for step in range(1, seq_count):
+            to_seq(h, step).wait_send()
+            to_seq(h, step).wait_recv()
+        to_self(h).wait()
+        return carry
+
+    lax.fori_loop(0, heads, drain, 0)
+
+
+def per_device_fused(queries, keys, values, span_order):
+    tokens, width = queries.shape[2], queries.shape[3]
+    heads = width // HD
+    seq_count = lax.axis_size("seq")
+    bias_rate = 1.0 / (2.0 * span_order.shape[0])
+    span = lax.axis_index("span")
+    own = lookup(span_order, jnp.reshape(span, (1,)))
+    other = lookup(span_order, jnp.reshape(1 - span, (1,)))
+    bias = (own - other).astype(jnp.float32) * jnp.float32(bias_rate)
+    shift = jnp.where(other <= own, bias * jnp.float32(LOG2E), jnp.float32(1e30))
+    whole = pl.BlockSpec(memory_space=pltpu.VMEM)
+    block = pltpu.VMEM((tokens, width), jnp.bfloat16)
+    pairs = pltpu.SemaphoreType.DMA((2, heads))
+    lines = pltpu.SemaphoreType.DMA((seq_count - 1, heads))
+    result = pl.pallas_call(
+        functools.partial(fused_kernel, heads, seq_count),
+        out_shape=jax.ShapeDtypeStruct((tokens // seq_count, width * seq_count), jnp.bfloat16),
+        in_specs=[pl.BlockSpec(memory_space=pltpu.SMEM), whole, whole, whole],
+        out_specs=whole,
+        scratch_shapes=[block] * 7 + [pairs] * 6 + [lines] * 2 + [pltpu.SemaphoreType.DMA((heads,))],
+        compiler_params=pltpu.CompilerParams(
+            collective_id=0, has_side_effects=True, vmem_limit_bytes=60 * 1024 * 1024
+        ),
+    )(
+        shift,
+        queries.reshape(tokens, width),
+        keys.reshape(tokens, width),
+        values.reshape(tokens, width),
+    )
+    return result.reshape(1, 1, tokens // seq_count, width * seq_count)
+
+
+def per_device(queries, keys, values, span_order):
+    tokens = queries.shape[2]
+    seq_count = lax.axis_size("seq")
+    part = tokens // seq_count
+    fits = (
+        lax.axis_size("span") == 2
+        and lax.axis_size("head") == 2
+        and tokens % ROWS == 0
+        and part % 16 == 0
+        and seq_count <= 8
+    )
+    run = per_device_fused if fits else per_device_general
+    return run(queries, keys, values, span_order)
+
+
 def solution(mesh):
     return jax.shard_map(
         per_device,

time: 447 us -> 132 us (0.30)
  Pallas kernels: 0 us -> 124 us
  matrix products: 112 us -> 0 us
  waiting for transfers between devices: 104 us -> 0 us
  other arithmetic: 104 us -> 1.38 us
  local copies, waits for them, and re-layouts: 57.9 us -> 3.13 us
  blocking collectives: 53.2 us -> 0 us
  between operations: 13.5 us -> 2.69 us
    pallas_call x0 -> x1, Pallas kernels: none -> 124 us  [per_device_fused(): pl.pallas_call(functools.partial(fused_kernel, heads, seq_count), out_sha...]
    dot_general x8 -> x0, matrix products: 112 us -> none  [the longest x4 66.3 us: advance(): jnp.einsum('qhd,khd->hqk', query_heads, key_block, preferred_element_type...]
    all_gather x2 -> x0, waiting for transfers between devices: 103 us -> none  [the longest x1 54.7 us: per_device(): lax.all_gather(keys, ('span', 'head'), axis=0, tiled=True)]
    reduce_sum x4 -> x0, other arithmetic: 86.4 us -> none  [advance(): totals = totals * shrink + jnp.sum(weights.astype(jnp.float32), axis=2)]
    all_to_all x1 -> x0, blocking collectives: 53.2 us -> none  [per_device(): lax.all_to_all(result, 'seq', split_axis=2, concat_axis=3, tiled=True)]
    all_gather x2 -> x0, local copies, waits for them, and re-layouts: 23 us -> none  [the longest x1 11.6 us: per_device(): lax.all_gather(keys, ('span', 'head'), axis=0, tiled=True)]
    unnamed x4 -> x0, other arithmetic: 13 us -> none
    unnamed x10 -> x1, local copies, waits for them, and re-layouts: 14.9 us -> 3.13 us
  transfers between devices with their start and end apart: 2 -> 0, of which waited for: 2 -> 0; matrix products, arithmetic and copies ran while one was open for 4% -> 0% of each run, Pallas kernels for 0% -> 0%
where the time goes in v1:
time: 132 us
  Pallas kernels  124 us (94%)
  local copies, waits for them, and re-layouts  3.13 us (2%)
  between operations  2.69 us (2%)
  other arithmetic  1.38 us (1%)
    pallas_call x1, Pallas kernels, per_device_fused(): pl.pallas_call(functools.partial(fused_kernel, heads, seq_count), out_sha...  124 us
    unnamed x1, local copies, waits for them, and re-layouts  3.13 us

profile of v1, /device:TPU:0, one launch (start us, length us, event | category | flops | bytes accessed | tf_op | source)
XLA Modules:
  0.0 131.6 jit_solution(12083324892041413281)
XLA Ops:
  0.0 1.4 %fusion.1 = (s32[]{:T(128)}, s32[]{:T(128)}) fusion(s32[2]{0:T(128)} %param.7, s32[]{:T(128)S(6)} %axis_index.15, s32[]{:T(128)S(6)} %sub.7), kind=kLoop, calls=%fused_computation.3 | loop fusion | flops 10 | bytes 24 | tf_op jit(solution)/shard_map/reduce_sum | solution.py:16
  4.1 124.4 %shard_map.46 = bf16[256,4096]{1,0:T(8,128)(2,1)} custom-call(f32[1]{0:T(128)} %bitcast.shift_ref, bf16[1024,1024]{1,0:T(8,128)(2,1)} %bitcast.6, bf16[1024,1024]{1,0:T(8,128)(2,1)} %bitcast.7, bf16[1024,1024]{1,0:T(8,128)(2,1)} %bitcast.8), custom_call_target="tpu_custom_call" | custom-call | tf_op jit(solution)/shard_map/pallas_call | solution.py:271
  128.5 3.1 %copy.6 = bf16[1,1,256,4096]{3,2,1,0:T(8,128)(2,1)} copy(bf16[1,1,256,4096]{3,2,1,0:T(8,128)(2,1)} %bitcast.5) | data formatting | bytes 4194304

commit v2 on v1

--- a/solution.py
+++ b/solution.py
@@ -110,12 +110,13 @@
 MESH = pl.DeviceIdType.MESH
 ROWS = 256
 LOG2E = 1.4426950408889634
+RATE = LOG2E / math.sqrt(HD)
 
 
 def fused_kernel(
-    heads, seq_count, shift_ref, q_ref, k_ref, v_ref, out_ref,
-    kp, vp, kx, vx, kd, vd, stage,
-    p_send, p_recv, x_send, x_recv, d_send, d_recv, z_send, z_recv, own_sem,
+    heads, seq_count, scalars_ref, q_ref, k_ref, v_ref, pay_ref, out_ref,
+    kp, vp, px, pd, own, own_lse, cross, cross_lse, back, back_lse, stage, jq, jk, jv,
+    p_send, p_recv, x_send, x_recv, d_send, d_recv, r_send, r_recv, z_send, z_recv, own_sem,
 ):
     rep, span = lax.axis_index("rep"), lax.axis_index("span")
     seq, core = lax.axis_index("seq"), lax.axis_index("head")
@@ -123,6 +124,7 @@
     across = (rep, 1 - span, seq, core)
     tokens, width = q_ref.shape
     part = tokens // seq_count
+    jobs = heads // 2
 
     def along(step):
         return lax.rem(seq + step, seq_count)
@@ -136,32 +138,48 @@
     def cols(h):
         return pl.ds(pl.multiple_of(h * HD, HD), HD)
 
-    def move(src, dst, send, recv, which, h, device):
+    def head_of(n):
+        return lax.rem(n, 2) * jobs + n // 2
+
+    def move(src, dst, send, recv, which, h, column, device):
         return pltpu.make_async_remote_copy(
-            src_ref=src.at[:, cols(h)],
-            dst_ref=dst.at[:, cols(h)],
+            src_ref=src.at[:, cols(column)],
+            dst_ref=dst.at[:, cols(column)],
             send_sem=send.at[which, h],
             recv_sem=recv.at[which, h],
             device_id=device,
             device_id_type=MESH,
         )
 
-    def to_across(h):
-        return (
-            move(k_ref, kx, x_send, x_recv, 0, h, across),
-            move(v_ref, vx, x_send, x_recv, 1, h, across),
-        )
-
     def to_partner(h):
         return (
-            move(k_ref, kp, p_send, p_recv, 0, h, partner),
-            move(v_ref, vp, p_send, p_recv, 1, h, partner),
-        )
-
-    def relay(h):
+            move(k_ref, kp, p_send, p_recv, 0, h, h, partner),
+            move(v_ref, vp, p_send, p_recv, 1, h, h, partner),
+        )
+
+    def to_across(j):
         return (
-            move(kx, kd, d_send, d_recv, 0, h, partner),
-            move(vx, vd, d_send, d_recv, 1, h, partner),
+            move(pay_ref, px, x_send, x_recv, 0, j, j, across),
+            move(pay_ref, px, x_send, x_recv, 1, j, j + jobs, across),
+        )
+
+    def relay(j):
+        return (
+            move(px, pd, d_send, d_recv, 0, j, j, partner),
+            move(px, pd, d_send, d_recv, 1, j, j + jobs, partner),
+        )
+
+    def give_back(j):
+        return (
+            move(cross, back, r_send, r_recv, 0, j, j, across),
+            pltpu.make_async_remote_copy(
+                src_ref=cross_lse.at[j],
+                dst_ref=back_lse.at[j],
+                send_sem=r_send.at[1, j],
+                recv_sem=r_recv.at[1, j],
+                device_id=across,
+                device_id_type=MESH,
+            ),
         )
 
     def out_cols(from_seq, h):
@@ -185,104 +203,190 @@
             own_sem.at[h],
         )
 
-    def launch(h, carry):
-        for copy in to_across(h) + to_partner(h):
-            copy.start()
-        return carry
-
-    lax.fori_loop(0, heads, launch, 0)
-
-    rate = jnp.float32(LOG2E / math.sqrt(HD))
-    shift = shift_ref[0]
-
-    def one_head(h, carry):
-        for copy in to_across(h):
-            copy.wait_recv()
-        for copy in relay(h):
-            copy.start()
-        for copy in to_partner(h):
-            copy.wait_recv()
-        for copy in relay(h):
-            copy.wait_recv()
-
-        def tile(t, inner):
-            rows = pl.ds(pl.multiple_of(t * ROWS, ROWS), ROWS)
-            query = q_ref[rows, cols(h)]
-
-            def score(ref):
-                return lax.dot_general(
-                    query, ref[:, cols(h)], (((1,), (1,)), ((), ())),
-                    preferred_element_type=jnp.float32,
-                )
-
-            near = [score(k_ref), score(kp)]
-            far = [score(kx), score(kd)]
-            near_max = jnp.max(jnp.maximum(near[0], near[1]), axis=1, keepdims=True) * rate
-            far_max = jnp.max(jnp.maximum(far[0], far[1]), axis=1, keepdims=True) * rate
-            top = jnp.maximum(near_max, far_max - shift)
-            far_top = top + shift
-            total = None
-            ones = jnp.ones((tokens, HD), jnp.bfloat16)
-            for scores, offset, ref in (
-                (near[0], top, v_ref), (near[1], top, vp),
-                (far[0], far_top, vx), (far[1], far_top, vd),
-            ):
-                weights = jnp.exp2(scores * rate - offset).astype(jnp.bfloat16)
-                value = jnp.concatenate([ref[:, cols(h)], ones], axis=1)
-                term = jnp.dot(weights, value, preferred_element_type=jnp.float32)
-                total = term if total is None else total + term
-            stage[rows, cols(h)] = (total[:, :HD] / total[:, HD:]).astype(jnp.bfloat16)
-            return inner
-
-        lax.fori_loop(0, tokens // ROWS, tile, 0)
+    def spread(h):
         for step in range(1, seq_count):
             to_seq(h, step).start()
         to_self(h).start()
-        return carry
-
-    lax.fori_loop(0, heads, one_head, 0)
+
+    def launch(n, carry):
+        for copy in to_partner(head_of(n)):
+            copy.start()
+        return carry
+
+    def launch_across(j, carry):
+        for copy in to_across(j):
+            copy.start()
+        return carry
+
+    lax.fori_loop(0, jobs, launch_across, 0)
+    lax.fori_loop(0, heads, launch, 0)
+
+    shift = scalars_ref[0]
+    higher = scalars_ref[1]
+    rate = jnp.float32(RATE)
+
+    def attend_rows(query, key_blocks, value_blocks):
+        scores = [
+            lax.dot_general(
+                query, key, (((1,), (1,)), ((), ())), preferred_element_type=jnp.float32
+            )
+            for key in key_blocks
+        ]
+        top = jnp.max(jnp.maximum(scores[0], scores[1]), axis=1, keepdims=True) * rate
+        ones = jnp.ones((tokens, HD), jnp.bfloat16)
+        total = None
+        for score, value in zip(scores, value_blocks):
+            weights = jnp.exp2(score * rate - top).astype(jnp.bfloat16)
+            term = jnp.dot(
+                weights, jnp.concatenate([value, ones], axis=1),
+                preferred_element_type=jnp.float32,
+            )
+            total = term if total is None else total + term
+        sums = total[:, HD:]
+        return total[:, :HD] / sums, top + jnp.log(sums) * jnp.float32(LOG2E)
+
+    def merge(near, near_lse, far, far_lse):
+        far_lse = far_lse - shift
+        top = jnp.maximum(near_lse, far_lse)
+        near_part, far_part = jnp.exp2(near_lse - top), jnp.exp2(far_lse - top)
+        mixed = (near * near_part + far * far_part) / (near_part + far_part)
+        return mixed.astype(jnp.bfloat16)
+
+    def choose(first, second):
+        picked = first.astype(jnp.float32) * higher + second.astype(jnp.float32) * (1.0 - higher)
+        return picked.astype(jnp.bfloat16)
+
+    def step(n, carry):
+        @pl.when(n < heads)
+        def own_job():
+            h = head_of(n)
+            for copy in to_partner(h):
+                copy.wait_recv()
+            for t in range(tokens // ROWS):
+                rows = pl.ds(t * ROWS, ROWS)
+                result, lse = attend_rows(
+                    q_ref[rows, cols(h)],
+                    (k_ref[:, cols(h)], kp[:, cols(h)]),
+                    (v_ref[:, cols(h)], vp[:, cols(h)]),
+                )
+                own[rows, cols(h)] = result
+                own_lse[rows, cols(h)] = lse
+
+        @pl.when(lax.rem(n, 2) == 1)
+        def pass_on():
+            j = n // 2
+            for copy in to_across(j):
+                copy.wait_recv()
+            for copy in relay(j):
+                copy.start()
+
+        @pl.when(jnp.logical_and(lax.rem(n, 2) == 0, n > 0))
+        def cross_job():
+            j = n // 2 - 1
+            b = j + jobs
+            for copy in relay(j):
+                copy.wait_recv()
+            jq[...] = choose(q_ref[:, cols(j)], px[:, cols(j)])
+            jk[0] = choose(px[:, cols(j)], k_ref[:, cols(b)])
+            jk[1] = choose(pd[:, cols(j)], kp[:, cols(b)])
+            jv[0] = choose(px[:, cols(b)], v_ref[:, cols(b)])
+            jv[1] = choose(pd[:, cols(b)], vp[:, cols(b)])
+            for t in range(tokens // ROWS):
+                rows = pl.ds(t * ROWS, ROWS)
+                result, lse = attend_rows(jq[rows, :], (jk[0], jk[1]), (jv[0], jv[1]))
+                cross[rows, cols(j)] = result.astype(jnp.bfloat16)
+                cross_lse[j, :, rows] = lse.T[:8, :]
+                stage[rows, cols(j)] = merge(
+                    own[rows, cols(j)], own_lse[rows, cols(j)], result, lse
+                )
+            for copy in give_back(j):
+                copy.start()
+            spread(j)
+
+        return carry
+
+    lax.fori_loop(0, heads + 1, step, 0)
+
+    def complete(j, carry):
+        b = j + jobs
+        for copy in give_back(j):
+            copy.wait_recv()
+        for t in range(tokens // ROWS):
+            rows = pl.ds(t * ROWS, ROWS)
+            lse = jnp.broadcast_to(back_lse[j, 0:1, rows], (HD, ROWS)).T
+            stage[rows, cols(b)] = merge(
+                own[rows, cols(b)], own_lse[rows, cols(b)],
+                back[rows, cols(j)].astype(jnp.float32), lse,
+            )
+        spread(b)
+        return carry
+
+    lax.fori_loop(0, jobs, complete, 0)
 
     def drain(h, carry):
-        for copy in to_across(h) + to_partner(h) + relay(h):
+        for copy in to_partner(h):
             copy.wait_send()
-        for step in range(1, seq_count):
-            to_seq(h, step).wait_send()
-            to_seq(h, step).wait_recv()
+        for hop in range(1, seq_count):
+            to_seq(h, hop).wait_send()
+            to_seq(h, hop).wait_recv()
         to_self(h).wait()
         return carry
 
+    def drain_jobs(j, carry):
+        for copy in to_across(j) + relay(j) + give_back(j):
+            copy.wait_send()
+        return carry
+
+    lax.fori_loop(0, jobs, drain_jobs, 0)
     lax.fori_loop(0, heads, drain, 0)
 
 
 def per_device_fused(queries, keys, values, span_order):
     tokens, width = queries.shape[2], queries.shape[3]
     heads = width // HD
+    jobs = heads // 2
+    half = jobs * HD
     seq_count = lax.axis_size("seq")
     bias_rate = 1.0 / (2.0 * span_order.shape[0])
     span = lax.axis_index("span")
     own = lookup(span_order, jnp.reshape(span, (1,)))
     other = lookup(span_order, jnp.reshape(1 - span, (1,)))
     bias = (own - other).astype(jnp.float32) * jnp.float32(bias_rate)
-    shift = jnp.where(other <= own, bias * jnp.float32(LOG2E), jnp.float32(1e30))
+    higher = other <= own
+    shift = jnp.where(higher, bias * jnp.float32(LOG2E), jnp.float32(1e30))
+    scalars = jnp.concatenate([shift, higher.astype(jnp.float32)])
+    query, key, value = (a.reshape(tokens, width) for a in (queries, keys, values))
+    payload = jnp.where(
+        higher[0],
+        jnp.concatenate([query[:, half:], query[:, :half]], axis=1),
+        jnp.concatenate([key[:, :half], value[:, :half]], axis=1),
+    )
     whole = pl.BlockSpec(memory_space=pltpu.VMEM)
     block = pltpu.VMEM((tokens, width), jnp.bfloat16)
+    wide = pltpu.VMEM((tokens, width), jnp.float32)
+    narrow = pltpu.VMEM((tokens, half), jnp.bfloat16)
+    rows = pltpu.VMEM((jobs, 8, tokens), jnp.float32)
+    both = pltpu.VMEM((2, tokens, HD), jnp.bfloat16)
     pairs = pltpu.SemaphoreType.DMA((2, heads))
+    few = pltpu.SemaphoreType.DMA((2, jobs))
     lines = pltpu.SemaphoreType.DMA((seq_count - 1, heads))
     result = pl.pallas_call(
         functools.partial(fused_kernel, heads, seq_count),
         out_shape=jax.ShapeDtypeStruct((tokens // seq_count, width * seq_count), jnp.bfloat16),
-        in_specs=[pl.BlockSpec(memory_space=pltpu.SMEM), whole, whole, whole],
+        in_specs=[pl.BlockSpec(memory_space=pltpu.SMEM), whole, whole, whole, whole],
         out_specs=whole,
-        scratch_shapes=[block] * 7 + [pairs] * 6 + [lines] * 2 + [pltpu.SemaphoreType.DMA((heads,))],
+        scratch_shapes=[block] * 4
+        + [wide] * 2
+        + [narrow, rows, narrow, rows, block]
+        + [pltpu.VMEM((tokens, HD), jnp.bfloat16), both, both]
+        + [pairs] * 2
+        + [few] * 6
+        + [lines] * 2
+        + [pltpu.SemaphoreType.DMA((heads,))],
         compiler_params=pltpu.CompilerParams(
             collective_id=0, has_side_effects=True, vmem_limit_bytes=60 * 1024 * 1024
         ),
-    )(
-        shift,
-        queries.reshape(tokens, width),
-        keys.reshape(tokens, width),
-        values.reshape(tokens, width),
-    )
+    )(scalars, query, key, value, payload)
     return result.reshape(1, 1, tokens // seq_count, width * seq_count)
 
 
@@ -295,6 +399,7 @@
         and lax.axis_size("head") == 2
         and tokens % ROWS == 0
         and part % 16 == 0
+        and queries.shape[3] % (2 * HD) == 0
         and seq_count <= 8
     )
     run = per_device_fused if fits else per_device_general

time: 132 us -> 104 us (0.79)
  Pallas kernels: 124 us -> 91.5 us
  other arithmetic: 1.38 us -> 4.07 us
  local copies, waits for them, and re-layouts: 3.13 us -> 5.15 us
    pallas_call x1, Pallas kernels: 124 us -> 91.5 us  [per_device_fused(): pl.pallas_call(functools.partial(fused_kernel, heads, seq_count), out_sha...]
    select_n x0 -> x1, other arithmetic: none -> 1.95 us  [per_device_fused(): jnp.where(higher[0], jnp.concatenate([query[:, half:], query[:, :half]],...]
    slice x0 -> x3, local copies, waits for them, and re-layouts: none -> 1.68 us  [the longest x1 1.44 us: per_device_fused(): key[:, :half]]
    unnamed x1 -> x5, local copies, waits for them, and re-layouts: 3.13 us -> 3.47 us
where the time goes in v2:
time: 104 us; the launch traced here: 103 us
  Pallas kernels  91.5 us (88%)
  local copies, waits for them, and re-layouts  5.15 us (5%)
  other arithmetic  4.07 us (4%)
  between operations  2.71 us (3%)
    pallas_call x1, Pallas kernels, per_device_fused(): pl.pallas_call(functools.partial(fused_kernel, heads, seq_count), out_sha...  91.5 us
    unnamed x5, local copies, waits for them, and re-layouts  3.47 us

profile of v2, /device:TPU:0, one launch (start us, length us, event | category | flops | bytes accessed | tf_op | source)
XLA Modules:
  0.0 103.5 jit_solution(12894445215536127191)
XLA Ops:
  0.0 0.0 copy-start.1
  0.0 1.5 %fusion.1 = (s32[]{:T(128)}, s32[]{:T(128)}) fusion(s32[2]{0:T(128)} %param.7, s32[]{:T(128)S(6)} %axis_index.15, s32[]{:T(128)S(6)} %sub.7), kind=kLoop, calls=%fused_computation.4 | loop fusion | flops 10 | bytes 24 | tf_op jit(solution)/shard_map/reduce_sum | solution.py:16
  4.2 0.6 pad_maximum_fusion.scalars_ref
  4.8 0.0 copy-start
  4.8 1.4 %slice.18 = bf16[1024,512]{1,0:T(8,128)(2,1)S(1)} slice(bf16[1024,1024]{1,0:T(8,128)(2,1)} %bitcast.9), slice={[0:1024], [0:512]} | slice | bytes 2097152 | tf_op jit(solution)/shard_map/slice | solution.py:362
  6.2 0.0 copy-done.1
  6.3 0.1 slice.19
  6.4 0.3 copy-done
  6.7 0.1 fusion.2
  6.8 1.9 %maximum_select_fusion.pay_ref = bf16[1024,1024]{1,0:T(8,128)(2,1)} fusion(bf16[1024,512]{1,0:T(8,128)(2,1)S(1)} %get-tuple-element.8, bf16[1024,512]{1,0:T(8,128)(2,1)S(1)} %get-tuple-element.7, bf16[1024,512]{1,0:T(8,128)(2,1)S(1)} %slice.19, bf16[1024,512]{1,0:T(8,128)(2,1)S(1)} %slice.18, pred[]{:T(512)S(6)} %le.4), kind=kLoop, calls=%fused_computation | loop fusion | flops 9437184 | bytes 6291457 | tf_op jit(solution)/shard_map/jit(_where)/select_n | solution.py:359
  8.8 91.5 %shard_map.46 = bf16[256,4096]{1,0:T(8,128)(2,1)} custom-call(f32[2]{0:T(128)} %pad_maximum_fusion.scalars_ref, bf16[1024,1024]{1,0:T(8,128)(2,1)} %bitcast.6, bf16[1024,1024]{1,0:T(8,128)(2,1)} %bitcast.10, bf16[1024,1024]{1,0:T(8,128)(2,1)} %bitcast.11, bf16[1024,1024]{1,0:T(8,128)(2,1)} %maximum_select_fusion.pay_ref), custom_call_target="tpu_custom_call" | custom-call | tf_op jit(solution)/shard_map/pallas_call | solution.py:373
  100.3 3.1 %copy.6 = bf16[1,1,256,4096]{3,2,1,0:T(8,128)(2,1)} copy(bf16[1,1,256,4096]{3,2,1,0:T(8,128)(2,1)} %bitcast.8) | data formatting | bytes 4194304
Async XLA Ops:
  0.0 6.3 %copy-start.1 = (bf16[1,1,1024,1024]{3,2,1,0:T(8,128)(2,1)S(1)}, bf16[1,1,1024,1024]{3,2,1,0:T(8,128)(2,1)}, u32[]{:S(2)}) copy-start(bf16[1,1,1024,1024]{3,2,1,0:T(8,128)(2,1)} %param.6) | copy-start | bytes 6291460
  4.8 1.9 %copy-start = (bf16[1,1,1024,1024]{3,2,1,0:T(8,128)(2,1)S(1)}, bf16[1,1,1024,1024]{3,2,1,0:T(8,128)(2,1)}, u32[]{:S(2)}) copy-start(bf16[1,1,1024,1024]{3,2,1,0:T(8,128)(2,1)} %param.4) | copy-start | bytes 6291460

commit v3 on v2

--- a/solution.py
+++ b/solution.py
@@ -114,8 +114,8 @@
 
 
 def fused_kernel(
-    heads, seq_count, scalars_ref, q_ref, k_ref, v_ref, pay_ref, out_ref,
-    kp, vp, px, pd, own, own_lse, cross, cross_lse, back, back_lse, stage, jq, jk, jv,
+    heads, seq_count, scalars_ref, q_ref, k_ref, v_ref, out_ref,
+    kp, vp, px, pd, own, own_lse, cross, cross_lse, back, back_lse, stage, jq, jk, jv, pay_ref,
     p_send, p_recv, x_send, x_recv, d_send, d_recv, r_send, r_recv, z_send, z_recv, own_sem,
 ):
     rep, span = lax.axis_index("rep"), lax.axis_index("span")
@@ -213,17 +213,24 @@
             copy.start()
         return carry
 
-    def launch_across(j, carry):
-        for copy in to_across(j):
-            copy.start()
-        return carry
-
-    lax.fori_loop(0, jobs, launch_across, 0)
-    lax.fori_loop(0, heads, launch, 0)
-
     shift = scalars_ref[0]
     higher = scalars_ref[1]
     rate = jnp.float32(RATE)
+
+    def choose(first, second):
+        picked = first.astype(jnp.float32) * higher + second.astype(jnp.float32) * (1.0 - higher)
+        return picked.astype(jnp.bfloat16)
+
+    def launch_across(j, carry):
+        b = j + jobs
+        pay_ref[:, cols(j)] = choose(q_ref[:, cols(b)], k_ref[:, cols(j)])
+        pay_ref[:, cols(b)] = choose(q_ref[:, cols(j)], v_ref[:, cols(j)])
+        for copy in to_across(j):
+            copy.start()
+        return carry
+
+    lax.fori_loop(0, heads, launch, 0)
+    lax.fori_loop(0, jobs, launch_across, 0)
 
     def attend_rows(query, key_blocks, value_blocks):
         scores = [
@@ -252,10 +259,6 @@
         mixed = (near * near_part + far * far_part) / (near_part + far_part)
         return mixed.astype(jnp.bfloat16)
 
-    def choose(first, second):
-        picked = first.astype(jnp.float32) * higher + second.astype(jnp.float32) * (1.0 - higher)
-        return picked.astype(jnp.bfloat16)
-
     def step(n, carry):
         @pl.when(n < heads)
         def own_job():
@@ -295,7 +298,7 @@
                 rows = pl.ds(t * ROWS, ROWS)
                 result, lse = attend_rows(jq[rows, :], (jk[0], jk[1]), (jv[0], jv[1]))
                 cross[rows, cols(j)] = result.astype(jnp.bfloat16)
-                cross_lse[j, :, rows] = lse.T[:8, :]
+                cross_lse[j, :, rows] = lse.T[:1, :]
                 stage[rows, cols(j)] = merge(
                     own[rows, cols(j)], own_lse[rows, cols(j)], result, lse
                 )
@@ -313,7 +316,7 @@
             copy.wait_recv()
         for t in range(tokens // ROWS):
             rows = pl.ds(t * ROWS, ROWS)
-            lse = jnp.broadcast_to(back_lse[j, 0:1, rows], (HD, ROWS)).T
+            lse = jnp.broadcast_to(back_lse[j, :, rows], (HD, ROWS)).T
             stage[rows, cols(b)] = merge(
                 own[rows, cols(b)], own_lse[rows, cols(b)],
                 back[rows, cols(j)].astype(jnp.float32), lse,
@@ -356,16 +359,11 @@
     shift = jnp.where(higher, bias * jnp.float32(LOG2E), jnp.float32(1e30))
     scalars = jnp.concatenate([shift, higher.astype(jnp.float32)])
     query, key, value = (a.reshape(tokens, width) for a in (queries, keys, values))
-    payload = jnp.where(
-        higher[0],
-        jnp.concatenate([query[:, half:], query[:, :half]], axis=1),
-        jnp.concatenate([key[:, :half], value[:, :half]], axis=1),
-    )
     whole = pl.BlockSpec(memory_space=pltpu.VMEM)
     block = pltpu.VMEM((tokens, width), jnp.bfloat16)
     wide = pltpu.VMEM((tokens, width), jnp.float32)
     narrow = pltpu.VMEM((tokens, half), jnp.bfloat16)
-    rows = pltpu.VMEM((jobs, 8, tokens), jnp.float32)
+    rows = pltpu.VMEM((jobs, 1, tokens), jnp.float32)
     both = pltpu.VMEM((2, tokens, HD), jnp.bfloat16)
     pairs = pltpu.SemaphoreType.DMA((2, heads))
     few = pltpu.SemaphoreType.DMA((2, jobs))
@@ -373,12 +371,12 @@
     result = pl.pallas_call(
         functools.partial(fused_kernel, heads, seq_count),
         out_shape=jax.ShapeDtypeStruct((tokens // seq_count, width * seq_count), jnp.bfloat16),
-        in_specs=[pl.BlockSpec(memory_space=pltpu.SMEM), whole, whole, whole, whole],
+        in_specs=[pl.BlockSpec(memory_space=pltpu.SMEM), whole, whole, whole],
         out_specs=whole,
         scratch_shapes=[block] * 4
         + [wide] * 2
         + [narrow, rows, narrow, rows, block]
-        + [pltpu.VMEM((tokens, HD), jnp.bfloat16), both, both]
+        + [pltpu.VMEM((tokens, HD), jnp.bfloat16), both, both, block]
         + [pairs] * 2
         + [few] * 6
         + [lines] * 2
@@ -386,7 +384,7 @@
         compiler_params=pltpu.CompilerParams(
             collective_id=0, has_side_effects=True, vmem_limit_bytes=60 * 1024 * 1024
         ),
-    )(scalars, query, key, value, payload)
+    )(scalars, query, key, value)
     return result.reshape(1, 1, tokens // seq_count, width * seq_count)
 
 

time: 104 us -> 99.2 us (0.954)
  other arithmetic: 4.07 us -> 1.97 us
  local copies, waits for them, and re-layouts: 5.15 us -> 3.13 us
    select_n x1 -> x0, other arithmetic: 1.95 us -> none  [per_device_fused(): jnp.where(higher[0], jnp.concatenate([query[:, half:], query[:, :half]],...]
    slice x3 -> x0, local copies, waits for them, and re-layouts: 1.68 us -> none  [the longest x1 1.44 us: per_device_fused(): key[:, :half]]
    unnamed x5 -> x1, local copies, waits for them, and re-layouts: 3.47 us -> 3.13 us
where the time goes in v3:
time: 99.2 us; the launch traced here: 99 us
  Pallas kernels  91.3 us (92%)
  local copies, waits for them, and re-layouts  3.13 us (3%)
  between operations  2.69 us (3%)
  other arithmetic  1.97 us (2%)
    pallas_call x1, Pallas kernels, per_device_fused(): pl.pallas_call(functools.partial(fused_kernel, heads, seq_count), out_sha...  91.3 us
    unnamed x1, local copies, waits for them, and re-layouts  3.13 us

profile of v3, /device:TPU:0, one launch (start us, length us, event | category | flops | bytes accessed | tf_op | source)
XLA Modules:
  0.0 99.0 jit_solution(12696693080882942008)
XLA Ops:
  0.0 1.4 %fusion.1 = (s32[]{:T(128)}, s32[]{:T(128)}) fusion(s32[2]{0:T(128)} %param.7, s32[]{:T(128)S(6)} %axis_index.15, s32[]{:T(128)S(6)} %sub.7), kind=kLoop, calls=%fused_computation.3 | loop fusion | flops 10 | bytes 24 | tf_op jit(solution)/shard_map/reduce_sum | solution.py:16
  4.1 0.6 pad_maximum_fusion.scalars_ref
  4.7 91.3 %shard_map.46 = bf16[256,4096]{1,0:T(8,128)(2,1)} custom-call(f32[2]{0:T(128)} %pad_maximum_fusion.scalars_ref, bf16[1024,1024]{1,0:T(8,128)(2,1)} %bitcast.7, bf16[1024,1024]{1,0:T(8,128)(2,1)} %bitcast.8, bf16[1024,1024]{1,0:T(8,128)(2,1)} %bitcast.9), custom_call_target="tpu_custom_call" | custom-call | tf_op jit(solution)/shard_map/pallas_call | solution.py:371
  95.9 3.1 %copy.6 = bf16[1,1,256,4096]{3,2,1,0:T(8,128)(2,1)} copy(bf16[1,1,256,4096]{3,2,1,0:T(8,128)(2,1)} %bitcast.6) | data formatting | bytes 4194304

commit v4 on v3

--- a/solution.py
+++ b/solution.py
@@ -372,7 +372,7 @@
         functools.partial(fused_kernel, heads, seq_count),
         out_shape=jax.ShapeDtypeStruct((tokens // seq_count, width * seq_count), jnp.bfloat16),
         in_specs=[pl.BlockSpec(memory_space=pltpu.SMEM), whole, whole, whole],
-        out_specs=whole,
+        out_specs=pl.BlockSpec(memory_space=pl.ANY),
         scratch_shapes=[block] * 4
         + [wide] * 2
         + [narrow, rows, narrow, rows, block]

time: 99.2 us -> 97.9 us (0.987)
  Pallas kernels: 91.3 us -> 90 us
    pallas_call x1, Pallas kernels: 91.3 us -> 90 us  [per_device_fused(): pl.pallas_call(functools.partial(fused_kernel, heads, seq_count), out_sha...]
where the time goes in v4:
time: 97.9 us; the launch traced here: 97.8 us
  Pallas kernels  90 us (92%)
  local copies, waits for them, and re-layouts  3.13 us (3%)
  between operations  2.69 us (3%)
  other arithmetic  1.97 us (2%)
    pallas_call x1, Pallas kernels, per_device_fused(): pl.pallas_call(functools.partial(fused_kernel, heads, seq_count), out_sha...  90 us
    unnamed x1, local copies, waits for them, and re-layouts  3.13 us

profile of v4, /device:TPU:0, one launch (start us, length us, event | category | flops | bytes accessed | tf_op | source)
XLA Modules:
  0.0 97.8 jit_solution(14898394305963693387)
XLA Ops:
  0.0 1.4 %fusion.1 = (s32[]{:T(128)}, s32[]{:T(128)}) fusion(s32[2]{0:T(128)} %param.7, s32[]{:T(128)S(6)} %axis_index.15, s32[]{:T(128)S(6)} %sub.7), kind=kLoop, calls=%fused_computation.3 | loop fusion | flops 10 | bytes 24 | tf_op jit(solution)/shard_map/reduce_sum | solution.py:16
  4.1 0.6 pad_maximum_fusion.scalars_ref
  4.7 90.0 %shard_map.46 = bf16[256,4096]{1,0:T(8,128)(2,1)} custom-call(f32[2]{0:T(128)} %pad_maximum_fusion.scalars_ref, bf16[1024,1024]{1,0:T(8,128)(2,1)} %bitcast.7, bf16[1024,1024]{1,0:T(8,128)(2,1)} %bitcast.8, bf16[1024,1024]{1,0:T(8,128)(2,1)} %bitcast.9), custom_call_target="tpu_custom_call" | custom-call | tf_op jit(solution)/shard_map/pallas_call | solution.py:371
  94.6 3.1 %copy.6 = bf16[1,1,256,4096]{3,2,1,0:T(8,128)(2,1)} copy(bf16[1,1,256,4096]{3,2,1,0:T(8,128)(2,1)} %bitcast.6) | data formatting | bytes 4194304
